TPU v7x, 512 devices: a whole 4x8x8 slice. The times are simulated.
512 devices in a mesh: row: 16 (over x_hi, z), col: 32 (over x_lo, y, core).
Axes of the slice: x: 4 (x_hi: 2, x_lo: 2; x = x_hi * 2 + x_lo), y: 8, z: 8, core: 2. Of those that a mesh axis runs over, the one named last changes fastest.
Arguments:
- slots: bfloat16 [3072, 128, 128], P(('row', 'col')), may hold values from -6 to 6
- block_list: int32 [3072], P(('row', 'col')), may hold values from -1 to 15, as said below
- metric: bfloat16 [8192, 4096], P('row', 'col'), may hold values from -0.125 to 0.125
Outputs:
- contracted: float32 [16384, 4096], P('row', 'col')
Inputs may be any that keep to these rules, and one draw needn't show every extreme that they name: `block_list`: the live entries of one device's 6 slots come first and name distinct blocks; -1 marks an unused slot; every device has at least 3 live slots and some device has all 6 live.
All inputs are finite; a program needn't handle non-finite values.
Results may differ from a plain program's by a relative error of at most 0.0003.
Values may be sent and summed in bfloat16 or wider, within the bound.
No kernel may reach another device: no remote copies, remote signals or barrier semaphores. Data moves between devices by JAX's collectives and lax.ppermute only.
A program may use at most 128 MiB of HBM per device.

v0:
```python
import jax
import jax.numpy as jnp
from jax import lax
from jax.sharding import PartitionSpec as P

BLK = 128
PAIR_DEV = 1024


def sent_to_all(shard, axis):
    copies = jnp.broadcast_to(shard, (lax.axis_size(axis), *shard.shape))
    return lax.all_to_all(copies, axis, split_axis=0, concat_axis=0, tiled=True)


def laid_out(tiles, dim):
    tiles = jnp.moveaxis(tiles, 0, dim)
    dims = tiles.shape
    return tiles.reshape(*dims[:dim], dims[dim] * dims[dim + 1], *dims[dim + 2 :])


def gathered_copies(shard, axis, dim):
    tiles = sent_to_all(shard, axis)
    return laid_out(tiles, dim)


def on_device(slots, block_list, metric):
    slot_count = block_list.shape[0]
    width = slots.shape[1]
    out_cols = metric.shape[1]
    metric_band = gathered_copies(metric, "row", 0)
    band_blocks = metric_band.shape[0] // width
    col_blocks = band_blocks // lax.axis_size("col")
    pair_blocks = PAIR_DEV // BLK
    metric_blocks = metric_band.reshape(band_blocks, width, out_cols)
    piece_slots = lax.all_gather(slots, "col", axis=0, tiled=True)
    piece_list = lax.all_gather(block_list, "col", axis=0, tiled=True)
    number = piece_list.shape[0]
    shard_of = jnp.arange(number, dtype=jnp.int32) // slot_count
    is_live = piece_list >= 0
    clipped = jnp.maximum(piece_list, 0)
    pair_block = clipped // col_blocks
    global_block = shard_of * col_blocks + clipped % col_blocks
    rows = metric_blocks[global_block]
    prod = jnp.einsum("sab,sbq->saq", piece_slots, rows, preferred_element_type=jnp.float32)
    placing = ((pair_block[:, None] == jnp.arange(pair_blocks)[None, :]) & is_live[:, None]).astype(
        jnp.float32
    )
    added = jnp.einsum("sp,saq->paq", placing, prod, precision=lax.Precision.HIGHEST)
    return added.reshape(pair_blocks * width, out_cols)


def solution(mesh):
    return jax.shard_map(
        on_device,
        mesh=mesh,
        in_specs=(P(("row", "col"), None, None), P(("row", "col")), P("row", "col")),
        out_specs=P("row", "col"),
        check_vma=False,
    )
```

profile of v0, /device:TPU:133, one launch (start us, length us, event | category | flops | bytes accessed | tf_op | source)
XLA Modules:
  0.0 136.9 jit_solution(17358989224031301215)
XLA Ops:
  6.5 0.0 copy-start
  6.5 0.0 all-gather.2.cloned.1.call-start
  6.5 0.7 all-gather.2.cloned.1.call-update
  7.3 2.6 %broadcast_in_dim.4 = bf16[16,512,128]{2,1,0:T(8,128)(2,1)} broadcast(bf16[512,128]{1,0:T(8,128)(2,1)} %param.5), dimensions={1,2} | broadcast | bytes 2228224 | tf_op jit(solution)/shard_map/broadcast_in_dim | solution.py:11
  9.9 10.9 %all-to-all-start = ((bf16[16,512,128]{2,1,0:T(8,128)(2,1)}), bf16[16,512,128]{2,1,0:T(8,128)(2,1)S(1)}, u32[]{:S(2)}, u32[]{:S(2)}) async-start(bf16[16,512,128]{2,1,0:T(8,128)(2,1)} %broadcast_in_dim.4), calls=%async_computation | async-start | bytes 4194304 | tf_op jit(solution)/shard_map/all_to_all | solution.py:12
  20.8 1.3 dynamic-slice
  22.7 0.0 copy-done
  22.8 0.2 dynamic-update-slice
  23.0 14.8 %all-reduce = s32[192]{0:T(256)S(1)} all-reduce(s32[192]{0:T(256)S(1)} %dynamic-update-slice), channel_id=1, replica_groups=mesh['row'=16,'col'=32] {'col'}, use_global_device_ids=true, to_apply=%add | all-reduce | flops 192 | bytes 1536
  37.8 29.6 %all-to-all-done = bf16[16,512,128]{2,1,0:T(8,128)(2,1)S(1)} async-done(((bf16[16,512,128]{2,1,0:T(8,128)(2,1)}), bf16[16,512,128]{2,1,0:T(8,128)(2,1)S(1)}, u32[]{:S(2)}, u32[]{:S(2)}) %all-to-all-start) | async-done | bytes 2097184 | tf_op jit(solution)/shard_map/all_to_all | solution.py:12
  67.5 8.1 %gather_fusion = bf16[192,128,128]{2,1,0:T(8,128)(2,1)} fusion(bf16[64,128,128]{2,1,0:T(8,128)(2,1)S(1)} %bitcast.11, s32[1024]{0:T(1024)S(1)} %pad_clamp_fusion), kind=kCustom, calls=%fused_computation | custom fusion | bytes 12583680 | tf_op jit(solution)/shard_map/gather | solution.py:43
  75.5 20.3 %all-gather.2.cloned.1.call-done = bf16[192,128,128]{2,1,0:T(8,128)(2,1)} async-done(((bf16[6,128,128]{2,1,0:T(8,128)(2,1)}), bf16[192,128,128]{2,1,0:T(8,128)(2,1)}) %all-gather.2.cloned.1.call-update) | async-done | bytes 6291472 | tf_op jit(solution)/shard_map/all_gather | solution.py:35
  95.8 13.7 %convolution_bitcast_fusion = f32[192,128,128]{1,2,0:T(8,128)} fusion(bf16[192,128,128]{2,1,0:T(8,128)(2,1)} %gather_fusion, bf16[192,128,128]{2,1,0:T(8,128)(2,1)} %all-gather.2.cloned.1.call-done), kind=kOutput, calls=%fused_computation.1 | convolution fusion | flops 805306368 | bytes 25165824 | tf_op jit(solution)/shard_map/sab,sbq->saq/dot_general | solution.py:44
  109.5 12.7 %copy.8 = f32[192,128,128]{2,0,1:T(8,128)} copy(f32[192,128,128]{1,2,0:T(8,128)} %convolution_bitcast_fusion) | data formatting | bytes 25165824 | tf_op jit(solution)/shard_map/sab,sbq->saq/dot_general | solution.py:44
  122.3 6.9 %fusion.2 = f32[8,128,128]{2,0,1:T(8,128)S(1)} fusion(f32[192,128,128]{2,0,1:T(8,128)} %copy.8, s32[192]{0:T(256)S(1)} %get-tuple-element.5, pred[192]{0:T(512)(128)(4,1)S(1)} %broadcast_compare_fusion), kind=kOutput, calls=%fused_computation.5 | convolution fusion | flops 301992960 | bytes 13108160 | tf_op jit(solution)/shard_map/sp,saq->paq/dot_general | solution.py:48
  129.2 0.9 copy.9
  (4 shorter events, 0.0 us)
Async XLA Ops:
  6.5 16.2 %copy-start = (s32[6]{0:T(128)S(1)}, s32[6]{0:T(128)}, u32[]{:S(2)}) copy-start(s32[6]{0:T(128)} %param.4) | copy-start | bytes 76
  6.5 89.3 %all-gather.2.cloned.1.call-start = ((), (), s32[]{:S(2)}) async-start(), calls=%async_computation.1 | async-start | bytes 6488064 | tf_op jit(solution)/shard_map/all_gather | solution.py:35
  9.9 57.6 %all-to-all-start = ((bf16[16,512,128]{2,1,0:T(8,128)(2,1)}), bf16[16,512,128]{2,1,0:T(8,128)(2,1)S(1)}, u32[]{:S(2)}, u32[]{:S(2)}) async-start(bf16[16,512,128]{2,1,0:T(8,128)(2,1)} %broadcast_in_dim.4), calls=%async_computation | async-start | bytes 4194304 | tf_op jit(solution)/shard_map/all_to_all | solution.py:12
Sparse Core Ops, SparseCore 0:
  9.5 86.3 all-gather.1
where the time goes:
time: 137 us
  waiting for transfers between devices  50.7 us (37%)
  local copies, waits for them, and re-layouts  25.8 us (19%)
  matrix products  20.6 us (15%)
  blocking collectives  14.8 us (11%)
  between operations  14.1 us (10%)
  starting transfers between devices  10.9 us (8%)
    all_to_all x1, waiting for transfers between devices, sent_to_all(): return lax.all_to_all(copies, axis, split_axis=0, concat_axis=0, tiled=True)  29.6 us
    all_gather x1, waiting for transfers between devices, on_device(): piece_slots = lax.all_gather(slots, 'col', axis=0, tiled=True)  20.3 us
    unnamed x1, blocking collectives  14.8 us
    dot_general x1, matrix products, on_device(): jnp.einsum('sab,sbq->saq', piece_slots, rows, preferred_element_type=jnp....  13.7 us
    dot_general x1, local copies, waits for them, and re-layouts, on_device(): jnp.einsum('sab,sbq->saq', piece_slots, rows, preferred_element_type=jnp....  12.7 us
    all_to_all x1, starting transfers between devices, sent_to_all(): return lax.all_to_all(copies, axis, split_axis=0, concat_axis=0, tiled=True)  10.9 us
    gather x1, local copies, waits for them, and re-layouts, on_device(): rows = metric_blocks[global_block]  8.05 us
    dot_general x1, matrix products, on_device(): jnp.einsum('sp,saq->paq', placing, prod, precision=lax.Precision.HIGHEST)  6.92 us
  transfers between devices with their start and end apart: 2, of which 2 were waited for; matrix products, arithmetic and copies ran while one was open for 9% of the time, Pallas kernels for 0%

commit v1 on v0

--- a/solution.py
+++ b/solution.py
@@ -32,7 +32,10 @@
     col_blocks = band_blocks // lax.axis_size("col")
     pair_blocks = PAIR_DEV // BLK
     metric_blocks = metric_band.reshape(band_blocks, width, out_cols)
-    piece_slots = lax.all_gather(slots, "col", axis=0, tiled=True)
+    size = lax.axis_size("col")
+    shards = jnp.stack([slots for _ in range(size)])
+    shards = lax.all_to_all(shards, "col", split_axis=0, concat_axis=0)
+    piece_slots = jnp.concatenate(shards, axis=0)
     piece_list = lax.all_gather(block_list, "col", axis=0, tiled=True)
     number = piece_list.shape[0]
     shard_of = jnp.arange(number, dtype=jnp.int32) // slot_count

time: 137 us -> 269 us (1.96)
  the two profiles are of different devices: /device:TPU:133 before, /device:TPU:8 now
where the time goes in v1:
time: 269 us
  blocking collectives  211 us (78%)
  local copies, waits for them, and re-layouts  28.7 us (11%)
  matrix products  20.6 us (8%)
  starting transfers between devices  7.91 us (3%)
    unnamed x1, blocking collectives  147 us
    all_to_all x1, blocking collectives, sent_to_all(): return lax.all_to_all(copies, axis, split_axis=0, concat_axis=0, tiled=True)  63.6 us
    dot_general x1, matrix products, on_device(): jnp.einsum('sab,sbq->saq', piece_slots, rows, preferred_element_type=jnp....  13.7 us
    dot_general x1, local copies, waits for them, and re-layouts, on_device(): jnp.einsum('sab,sbq->saq', piece_slots, rows, preferred_element_type=jnp....  12.8 us
    gather x1, local copies, waits for them, and re-layouts, on_device(): rows = metric_blocks[global_block]  8 us
    all_to_all x1, starting transfers between devices, on_device(): shards = lax.all_to_all(shards, 'col', split_axis=0, concat_axis=0)  7.91 us
    dot_general x1, matrix products, on_device(): jnp.einsum('sp,saq->paq', placing, prod, precision=lax.Precision.HIGHEST)  6.89 us
  transfers between devices with their start and end apart: 1, of which 0 were waited for; matrix products, arithmetic and copies ran while one was open for 4% of the time, Pallas kernels for 0%

profile of v1, /device:TPU:8, one launch (start us, length us, event | category | flops | bytes accessed | tf_op | source)
XLA Modules:
  0.0 268.8 jit_solution(3402161775482614505)
XLA Ops:
  0.0 0.0 copy-start
  0.0 1.3 broadcast_in_dim.4
  1.4 63.6 %all_to_all.10 = bf16[16,512,128]{2,1,0:T(8,128)(2,1)S(1)} all-to-all(bf16[16,512,128]{2,1,0:T(8,128)(2,1)S(1)} %broadcast_in_dim.4), channel_id=1, replica_groups=mesh['row'=16,'col'=32] {'row'}, dimensions={0} | all-to-all | bytes 4194304 | tf_op jit(solution)/shard_map/all_to_all | solution.py:12
  64.9 0.0 copy-done
  64.9 4.2 %stack.2 = bf16[32,6,128,128]{3,2,1,0:T(8,128)(2,1)} broadcast(bf16[6,128,128]{2,1,0:T(8,128)(2,1)S(1)} %copy-done), dimensions={1,2,3} | broadcast | bytes 6488064 | tf_op jit(solution)/shard_map/stack | solution.py:36
  69.1 0.0 copy-start.1
  69.1 7.9 %all-to-all-start.1 = ((bf16[32,6,128,128]{3,2,1,0:T(8,128)(2,1)}), bf16[32,6,128,128]{3,2,1,0:T(8,128)(2,1)}, u32[]{:S(2)}, u32[]{:S(2)}) async-start(bf16[32,6,128,128]{3,2,1,0:T(8,128)(2,1)} %stack.2), calls=%async_computation.1 | async-start | bytes 12582912 | tf_op jit(solution)/shard_map/all_to_all | solution.py:37
  77.1 1.3 dynamic-slice
  79.0 0.0 copy-done.1
  79.0 0.2 dynamic-update-slice
  79.2 147.3 %all-reduce = s32[192]{0:T(256)S(1)} all-reduce(s32[192]{0:T(256)S(1)} %dynamic-update-slice), channel_id=1, replica_groups=mesh['row'=16,'col'=32] {'col'}, use_global_device_ids=true, to_apply=%add | all-reduce | flops 192 | bytes 1536
  226.6 8.0 %gather_fusion = bf16[192,128,128]{2,1,0:T(8,128)(2,1)} fusion(bf16[64,128,128]{2,1,0:T(8,128)(2,1)S(1)} %bitcast.12, s32[1024]{0:T(1024)S(1)} %pad_clamp_fusion), kind=kCustom, calls=%fused_computation | custom fusion | bytes 12583680 | tf_op jit(solution)/shard_map/gather | solution.py:46
  234.6 0.0 all-to-all-done.1
  234.6 13.7 %fusion.9 = f32[192,128,128]{2,1,0:T(8,128)} fusion(bf16[192,128,128]{2,1,0:T(8,128)(2,1)} %gather_fusion, bf16[192,128,128]{2,1,0:T(8,128)(2,1)} %bitcast.3), kind=kOutput, calls=%fused_computation.20 | convolution fusion | flops 805306368 | bytes 25165824 | tf_op jit(solution)/shard_map/sab,sbq->saq/dot_general | solution.py:47
  248.3 12.8 %copy.5 = f32[192,128,128]{1,0,2:T(8,128)} copy(f32[192,128,128]{2,1,0:T(8,128)} %fusion.9) | data formatting | bytes 25165824 | tf_op jit(solution)/shard_map/sab,sbq->saq/dot_general | solution.py:47
  261.0 6.9 %fusion = f32[8,128,128]{2,0,1:T(8,128)S(1)} fusion(f32[192,128,128]{1,0,2:T(8,128)} %copy.5, s32[192]{0:T(256)S(1)} %get-tuple-element.5, pred[192]{0:T(512)(128)(4,1)S(1)} %broadcast_compare_fusion), kind=kOutput, calls=%fused_computation.1 | convolution fusion | flops 301992960 | bytes 13108160 | tf_op jit(solution)/shard_map/sp,saq->paq/dot_general | solution.py:51
  267.9 0.9 copy.4
  (4 shorter events, 0.0 us)
Async XLA Ops:
  0.0 64.9 %copy-start = (bf16[6,128,128]{2,1,0:T(8,128)(2,1)S(1)}, bf16[6,128,128]{2,1,0:T(8,128)(2,1)}, u32[]{:S(2)}) copy-start(bf16[6,128,128]{2,1,0:T(8,128)(2,1)} %param.3) | copy-start | bytes 589828
  69.1 9.9 %copy-start.1 = (s32[6]{0:T(128)S(1)}, s32[6]{0:T(128)}, u32[]{:S(2)}) copy-start(s32[6]{0:T(128)} %param.4) | copy-start | bytes 76
  69.1 165.4 %all-to-all-start.1 = ((bf16[32,6,128,128]{3,2,1,0:T(8,128)(2,1)}), bf16[32,6,128,128]{3,2,1,0:T(8,128)(2,1)}, u32[]{:S(2)}, u32[]{:S(2)}) async-start(bf16[32,6,128,128]{3,2,1,0:T(8,128)(2,1)} %stack.2), calls=%async_computation.1 | async-start | bytes 12582912 | tf_op jit(solution)/shard_map/all_to_all | solution.py:37
